TPU v7x, 512 devices: a whole 4x8x8 slice. The times are simulated.
512 devices in a mesh: expert: 32 (over y, x), tensor: 16 (over z, core).
Axes of the slice: x: 4, y: 8, z: 8, core: 2. Of those that a mesh axis runs over, the one named last changes fastest.
Arguments:
- residual: bfloat16 [2048, 7168], P('expert', 'tensor'), may hold values from -40 to 40
- attn_parts: bfloat16 [16, 2048, 7168], P('tensor', 'expert'), may hold values from -2 to 2
- norm_gain: bfloat16 [7168], P('tensor'), may hold values from 0.099609375 to 1.8984375
- routes: int32 [2048, 8], P('expert'), may hold values from 0 to 31, all different within a row; in each aligned block of 64 rows (0 to 63, 64 to 127, ...) at most 24 rows name the same one
- route_weights: float32 [2048, 8], P('expert'), may hold values from 0.05 to 0.6
- w_gate: bfloat16 [32, 7168, 2048], P('expert', None, 'tensor'), may hold values from -0.06023809 to 0.06023809
- w_gate_q: bfloat16 [32, 7168, 2048], P('expert', None, 'tensor'), may hold values from -0.09567226 to 0.09567226
Outputs:
- token_error: float32 [2048], P('expert')
- expert_error: float32 [32], P('expert')
- hess_diag: float32 [32, 7168], P('expert', 'tensor')
Inputs may be any that keep to these rules, and one draw needn't show every extreme that they name: `routes`: no expert is named by more than 24 of the rows of one device, and in every draw some expert is named by exactly 24 of them; the 8 experts of a token are distinct; every expert is named by some token.
All inputs are finite; a program needn't handle non-finite values.
Results may differ from a plain program's by a relative error of at most 0.0023.
Values may be sent and summed in bfloat16 or wider, within the bound.
A program may use at most 64 MiB of HBM per device.

v0:
```python
import jax
import jax.numpy as jnp
from jax import lax
from jax.sharding import PartitionSpec as P

D = 7168
FF = 2048
CAP = 24
epsilon = 1e-06


def per_device(residual, attn_parts, norm_gain, routes, route_weights, w_gate, w_gate_q):
    n_expert = lax.axis_size("expert")
    tok_count = residual.shape[0]
    local_cols = residual.shape[1]
    top_count = routes.shape[1]
    gain_local = norm_gain.astype(jnp.float32)[None, :]
    gain_full = lax.all_gather(norm_gain, "tensor", tiled=True).astype(jnp.float32)[None, :]
    summed = lax.psum_scatter(
        attn_parts[0].astype(jnp.float32).astype(jnp.bfloat16),
        "tensor",
        scatter_dimension=1,
        tiled=True,
    ).astype(jnp.float32)
    hidden = (residual.astype(jnp.float32) + summed).astype(jnp.bfloat16)
    expert_ids = jnp.arange(n_expert, dtype=jnp.int32)
    flat_routes = routes.reshape(-1)
    one_hot = (flat_routes[:, None] == expert_ids[None, :]).astype(jnp.int32)
    earlier = jnp.cumsum(one_hot, axis=0) - one_hot
    slot_index = jnp.sum(earlier * one_hot, axis=1)
    target = flat_routes * CAP + slot_index
    load_counts = jnp.sum(one_hot, axis=0)
    slot_ids = jnp.arange(n_expert * CAP, dtype=jnp.int32)
    placing = (slot_ids[:, None] == target[None, :]).reshape(n_expert * CAP, tok_count, top_count)
    dispatch = jnp.sum(placing.astype(jnp.int32), axis=2).astype(jnp.bfloat16)
    outgoing = jnp.dot(dispatch, hidden, preferred_element_type=jnp.float32).astype(jnp.bfloat16)
    outgoing = outgoing.reshape(n_expert, CAP, local_cols)
    count_rows = jnp.broadcast_to(
        load_counts.astype(jnp.bfloat16)[:, None, None], (n_expert, 1, local_cols)
    )
    outgoing = jnp.concatenate([outgoing, count_rows], axis=1)
    arrived = lax.all_to_all(outgoing, "expert", split_axis=0, concat_axis=0, tiled=True)
    arrived_counts = arrived[:, CAP, 0].astype(jnp.float32)
    own_block = arrived[:, :CAP, :].reshape(n_expert * CAP, local_cols)
    column_block = lax.all_gather(own_block, "tensor", axis=1, tiled=True)
    wide = column_block.astype(jnp.float32)
    scaling = lax.rsqrt(jnp.sum(wide * wide, axis=1, keepdims=True) / D + epsilon)
    normed = (wide * scaling * gain_full).astype(jnp.bfloat16)
    normed_local = (own_block.astype(jnp.float32) * scaling * gain_local).astype(jnp.bfloat16)
    full_acc = jnp.dot(normed, w_gate[0], preferred_element_type=jnp.float32)
    quant_acc = jnp.dot(normed, w_gate_q[0], preferred_element_type=jnp.float32)
    block_squares = jnp.einsum(
        "rc,rc->c", normed_local, normed_local, preferred_element_type=jnp.float32
    )
    total_load = jnp.sum(arrived_counts)
    hess_local = 2.0 * block_squares / total_load
    difference = full_acc - quant_acc
    err_part = (jnp.sum(difference * difference, axis=1) / FF).reshape(n_expert, 1, CAP)
    pow_part = (jnp.sum(full_acc * full_acc, axis=1) / FF).reshape(n_expert, 1, CAP)
    slots = lax.psum(jnp.concatenate([err_part, pow_part], axis=1), "tensor")
    expert_total = jnp.sum(slots[:, 0]) / (jnp.sum(slots[:, 1]) + epsilon)
    back = lax.all_to_all(slots, "expert", split_axis=0, concat_axis=0, tiled=True)
    token_err = jnp.take(back[:, 0].reshape(-1), target).reshape(tok_count, top_count)
    token_pow = jnp.take(back[:, 1].reshape(-1), target).reshape(tok_count, top_count)
    ratios = token_err / (token_pow + epsilon)
    token_error = jnp.sum(route_weights * ratios, axis=1)
    return (token_error, expert_total.reshape(1), hess_local.reshape(1, local_cols))


def solution(mesh):
    placed = (
        P("expert", "tensor"),
        P("tensor", "expert", None),
        P("tensor"),
        P("expert", None),
        P("expert", None),
        P("expert", None, "tensor"),
        P("expert", None, "tensor"),
    )
    return jax.shard_map(
        per_device,
        mesh=mesh,
        in_specs=placed,
        out_specs=(P("expert"), P("expert"), P("expert", "tensor")),
        check_vma=False,
    )
```

profile of v0, /device:TPU:2, one launch (start us, length us, event | category | flops | bytes accessed | tf_op | source)
XLA Modules:
  0.0 279.3 jit_solution(10890716168880705273)
XLA Ops:
  7.2 0.0 copy-start
  7.2 0.0 reduce-scatter.4.cloned.1.call-start
  7.2 0.0 copy-start.5
  7.2 2.8 copy.51
  10.0 0.0 copy-start.4
  10.0 0.0 reduce-scatter.4.cloned.1.call-update
  10.0 0.0 all-gather.2.cloned.1.call-start
  10.1 0.0 copy-done.5
  10.1 0.1 copy.36
  10.2 0.1 eq.40
  10.3 0.1 eq.44
  10.4 1.2 reduce-window.6
  11.5 0.2 slice_reduce_fusion
  11.8 0.2 fusion.28
  11.9 0.1 reduce_sum.93
  12.0 0.1 copy.39
  12.1 0.1 copy.40
  12.2 0.5 convert_reduce_fusion
  12.7 65.0 %reduce-scatter.4.cloned.1.call-done = bf16[448,64]{1,0:T(8,128)(2,1)} async-done(((bf16[7168,64]{1,0:T(8,128)(2,1)}), bf16[448,64]{1,0:T(8,128)(2,1)}) %reduce-scatter.4.cloned.1.call-update) | async-done | bytes 57360
  77.8 1.0 copy.52
  78.8 0.0 copy-done.4
  78.8 0.4 convolution_convert_fusion
  79.2 0.3 copy.41
  79.5 0.1 broadcast_in_dim.6
  79.6 0.2 pad_maximum_fusion
  79.8 34.8 %all_to_all.10 = bf16[32,25,448]{2,1,0:T(8,128)(2,1)S(1)} all-to-all(bf16[32,25,448]{2,1,0:T(8,128)(2,1)S(1)} %pad_maximum_fusion), channel_id=1, replica_groups=mesh['expert'=32,'tensor'=16] {'expert'}, dimensions={0} | all-to-all | bytes 1433600 | tf_op jit(solution)/shard_map/all_to_all | solution.py:42
  114.5 0.0 copy-start.3
  114.5 1.0 copy-done.3
  115.5 0.1 slice.37
  115.6 0.0 copy-start.2
  115.6 1.2 copy.42
  116.8 0.0 all-gather.2.cloned.1.call-update
  116.8 0.0 copy-done.7
  116.8 1.3 dynamic-slice
  118.8 0.3 dynamic-update-slice
  119.0 51.5 %all-reduce = bf16[7168]{0:T(1024)(128)(2,1)S(1)} all-reduce(bf16[7168]{0:T(1024)(128)(2,1)S(1)} %dynamic-update-slice), channel_id=1, replica_groups=mesh['expert'=32,'tensor'=16] {'tensor'}, use_global_device_ids=true, to_apply=%add | all-reduce | flops 7168 | bytes 28672
  170.5 0.0 copy-done.6
  170.5 0.1 copy.44
  170.6 1.5 fusion.30
  172.1 0.0 copy-done.2
  172.1 13.0 %all-gather.2.cloned.1.call-done = bf16[768,7168]{0,1:T(8,128)(2,1)} async-done(((bf16[768,448]{0,1:T(8,128)(2,1)}), bf16[768,7168]{0,1:T(8,128)(2,1)}) %all-gather.2.cloned.1.call-update) | async-done | bytes 11010064 | tf_op jit(solution)/shard_map/all_gather | solution.py:45
  185.1 6.5 %fusion = f32[768]{0:T(1024)S(1)} fusion(bf16[768,7168]{0,1:T(8,128)(2,1)} %all-gather.2.cloned.1.call-done), kind=kLoop, calls=%fused_computation.4 | loop fusion | flops 16514304 | bytes 11013120 | tf_op jit(solution)/shard_map/reduce_sum | solution.py:47
  191.6 1.5 fusion.9
  193.1 0.0 copy-done
  193.1 0.0 copy-done.1
  193.1 0.0 copy-start.8
  193.1 3.3 %multiply_reduce_fusion = (f32[768]{0:T(1024)S(1)}, f32[768,128]{0,1:T(8,128)S(1)}) fusion(bf16[1,7168,128]{2,1,0:T(8,128)(2,1)S(1)} %copy-done, bf16[768,7168]{0,1:T(8,128)(2,1)S(1)} %copy-done.1, f32[7168]{0:T(1024)S(1)} %convert_element_type.66, f32[768]{0:T(1024)S(1)} %add_rsqrt_fusion), kind=kOutput, calls=%fused_computation.22 | convolution fusion | flops 1431502080 | bytes 13273088 | tf_op jit(solution)/shard_map/dot_general | solution.py:50
  196.5 0.0 copy-done.8
  196.5 3.4 %fusion.20 = f32[768]{0:T(1024)S(1)} fusion(f32[768,128]{0,1:T(8,128)S(1)} %get-tuple-element.11, bf16[1,7168,128]{2,1,0:T(8,128)(2,1)S(1)} %copy-done.8, bf16[768,7168]{0,1:T(8,128)(2,1)S(1)} %copy-done.1, f32[7168]{0:T(1024)S(1)} %convert_element_type.66, f32[768]{0:T(1024)S(1)} %add_rsqrt_fusion), kind=kOutput, calls=%fused_computation.19 | convolution fusion | flops 1431600384 | bytes 13273088 | tf_op jit(solution)/shard_map/dot_general | solution.py:51
  199.8 0.1 div.34
  199.9 0.1 div.36
  200.0 46.7 %psum.7 = f32[32,2,24]{2,0,1:T(8,128)S(1)} all-reduce(f32[32,2,24]{2,0,1:T(8,128)S(1)} %pad_maximum_fusion.1), channel_id=1, replica_groups=mesh['expert'=32,'tensor'=16] {'tensor'}, use_global_device_ids=true, to_apply=%region_9.10 | all-reduce | flops 1536 | bytes 12288 | tf_op jit(solution)/shard_map/psum | solution.py:60
  246.7 0.6 copy.43
  247.4 9.8 %all-to-all-start.1 = ((f32[32,2,24]{2,1,0:T(2,128)}), f32[32,2,24]{2,1,0:T(2,128)S(1)}, u32[]{:S(2)}, u32[]{:S(2)}) async-start(f32[32,2,24]{2,1,0:T(2,128)} %copy.43), calls=%async_computation.1 | async-start | bytes 65536 | tf_op jit(solution)/shard_map/all_to_all | solution.py:62
  257.1 1.2 multiply_divide_fusion
  258.4 0.6 slice_reduce_fusion.1
  260.3 5.5 %all-to-all-done.1 = f32[32,2,24]{2,1,0:T(2,128)S(1)} async-done(((f32[32,2,24]{2,1,0:T(2,128)}), f32[32,2,24]{2,1,0:T(2,128)S(1)}, u32[]{:S(2)}, u32[]{:S(2)}) %all-to-all-start.1) | async-done | bytes 6176 | tf_op jit(solution)/shard_map/all_to_all | solution.py:62
  265.8 0.1 slice_reduce_fusion.4
  265.9 0.1 reshape_squeeze.6
  266.0 0.1 reshape_squeeze.7
  266.0 2.3 gather_fusion
  268.3 2.3 gather_fusion.1
  270.6 0.1 div.38
  270.7 0.6 multiply_reduce_fusion.1
  (18 shorter events, 0.1 us)
Async XLA Ops:
  7.2 186.0 %copy-start = (bf16[1,7168,128]{2,1,0:T(8,128)(2,1)S(1)}, bf16[1,7168,128]{2,1,0:T(8,128)(2,1)}, u32[]{:S(2)}) copy-start(bf16[1,7168,128]{2,1,0:T(8,128)(2,1)} %param.14) | copy-start | bytes 5505028
  7.2 70.6 %reduce-scatter.4.cloned.1.call-start = ((), (), s32[]{:S(2)}) async-start(), calls=%async_computation.4 | async-start | bytes 1949696
  7.2 2.8 %copy-start.5 = (s32[64,8]{0,1:T(8,128)S(1)}, s32[64,8]{0,1:T(8,128)}, u32[]{:S(2)}) copy-start(s32[64,8]{0,1:T(8,128)} %param.12) | copy-start | bytes 6148
  10.0 68.8 %copy-start.4 = (bf16[64,448]{1,0:T(8,128)(2,1)S(1)}, bf16[64,448]{1,0:T(8,128)(2,1)}, u32[]{:S(2)}) copy-start(bf16[64,448]{1,0:T(8,128)(2,1)} %param.9) | copy-start | bytes 172036
  10.0 175.1 %all-gather.2.cloned.1.call-start = ((), (), s32[]{:S(2)}) async-start(), calls=%async_computation.3 | async-start | bytes 11698176 | tf_op jit(solution)/shard_map/all_gather | solution.py:45
  114.5 1.0 copy-start.3
  115.5 1.3 copy-start.7
  115.5 55.0 %copy-start.6 = (f32[64,8]{0,1:T(8,128)S(1)}, f32[64,8]{0,1:T(8,128)}, u32[]{:S(2)}) copy-start(f32[64,8]{0,1:T(8,128)} %param.13) | copy-start | bytes 6148
  115.6 56.5 %copy-start.2 = (bf16[32,24,448]{2,1,0:T(8,128)(2,1)}, bf16[32,24,448]{2,1,0:T(8,128)(2,1)S(1)}, u32[]{:S(2)}) copy-start(bf16[32,24,448]{2,1,0:T(8,128)(2,1)S(1)} %slice.37) | copy-start | bytes 2064388
  185.1 8.0 %copy-start.1 = (bf16[768,7168]{0,1:T(8,128)(2,1)S(1)}, bf16[768,7168]{0,1:T(8,128)(2,1)}, u32[]{:S(2)}) copy-start(bf16[768,7168]{0,1:T(8,128)(2,1)} %all-gather.2.cloned.1.call-done) | copy-start | bytes 33030148
  193.1 3.3 %copy-start.8 = (bf16[1,7168,128]{2,1,0:T(8,128)(2,1)S(1)}, bf16[1,7168,128]{2,1,0:T(8,128)(2,1)}, u32[]{:S(2)}) copy-start(bf16[1,7168,128]{2,1,0:T(8,128)(2,1)} %param.15) | copy-start | bytes 5505028
  247.4 18.4 %all-to-all-start.1 = ((f32[32,2,24]{2,1,0:T(2,128)}), f32[32,2,24]{2,1,0:T(2,128)S(1)}, u32[]{:S(2)}, u32[]{:S(2)}) async-start(f32[32,2,24]{2,1,0:T(2,128)} %copy.43), calls=%async_computation.1 | async-start | bytes 65536 | tf_op jit(solution)/shard_map/all_to_all | solution.py:62
Sparse Core Ops, SparseCore 0:
  10.8 66.8 reduce-scatter.3
  116.9 68.1 all-gather.1
where the time goes:
time: 280 us; the launch traced here: 279 us
  blocking collectives  133 us (48%)
  waiting for transfers between devices  83.6 us (30%)
  between operations  17.4 us (6%)
  local copies, waits for them, and re-layouts  14.4 us (5%)
  other arithmetic  14.1 us (5%)
  starting transfers between devices  9.86 us (4%)
  matrix products  7.03 us (3%)
    unnamed x3, waiting for transfers between devices  65.1 us
    unnamed x1, blocking collectives  51.5 us
    psum x1, blocking collectives, per_device(): slots = lax.psum(jnp.concatenate([err_part, pow_part], axis=1), 'tensor')  46.7 us
    all_to_all x1, blocking collectives, per_device(): lax.all_to_all(outgoing, 'expert', split_axis=0, concat_axis=0, tiled=True)  34.8 us
    all_gather x1, waiting for transfers between devices, per_device(): column_block = lax.all_gather(own_block, 'tensor', axis=1, tiled=True)  13 us
    all_to_all x1, starting transfers between devices, per_device(): lax.all_to_all(slots, 'expert', split_axis=0, concat_axis=0, tiled=True)  9.77 us
    reduce_sum x1, other arithmetic, per_device(): jnp.sum(wide * wide, axis=1, keepdims=True) / D + epsilon  6.51 us
    unnamed x25, local copies, waits for them, and re-layouts  6.44 us
  transfers between devices with their start and end apart: 3, of which 3 were waited for; matrix products, arithmetic and copies ran while one was open for 3% of the time, Pallas kernels for 0%

commit v1 on v0

--- a/solution.py
+++ b/solution.py
@@ -42,7 +42,9 @@
     arrived = lax.all_to_all(outgoing, "expert", split_axis=0, concat_axis=0, tiled=True)
     arrived_counts = arrived[:, CAP, 0].astype(jnp.float32)
     own_block = arrived[:, :CAP, :].reshape(n_expert * CAP, local_cols)
-    column_block = lax.all_gather(own_block, "tensor", axis=1, tiled=True)
+    column_block = jnp.concatenate(
+        lax.all_to_all(jnp.stack([own_block] * lax.axis_size("tensor")), "tensor", 0, 0), axis=1
+    )
     wide = column_block.astype(jnp.float32)
     scaling = lax.rsqrt(jnp.sum(wide * wide, axis=1, keepdims=True) / D + epsilon)
     normed = (wide * scaling * gain_full).astype(jnp.bfloat16)

time: 280 us -> 502 us (1.79)
  blocking collectives: 133 us -> 359 us
  waiting for transfers between devices: 83.6 us -> 70.6 us
  other arithmetic: 14.1 us -> 19.7 us
    unnamed x1, blocking collectives: 51.5 us -> 278 us
    all_gather x1 -> x0, waiting for transfers between devices: 13 us -> none  [per_device(): column_block = lax.all_gather(own_block, 'tensor', axis=1, tiled=True)]
    convert_element_type x1, other arithmetic: 0.01 us -> 6.84 us  [per_device(): normed = (wide * scaling * gain_full).astype(jnp.bfloat16)]
    all_to_all x0 -> x1, starting transfers between devices: none -> 6.54 us  [per_device(): lax.all_to_all(jnp.stack([own_block] * lax.axis_size('tensor')), 'tensor'...]
    another operation x1 -> x3, local copies, waits for them, and re-layouts: 0.01 us -> 5.36 us  [the longest x2 5.36 us: per_device(): jnp.stack([own_block] * lax.axis_size('tensor'))]
    unnamed x3 -> x2, waiting for transfers between devices: 65.1 us -> 65.1 us
  transfers between devices with their start and end apart: 3 -> 3, of which waited for: 3 -> 2; matrix products, arithmetic and copies ran while one was open for 3% -> 2% of each run, Pallas kernels for 0% -> 0%
where the time goes in v1:
time: 502 us; the launch traced here: 501 us
  blocking collectives  359 us (72%)
  waiting for transfers between devices  70.6 us (14%)
  other arithmetic  19.7 us (4%)
  local copies, waits for them, and re-layouts  18.7 us (4%)
  between operations  17.4 us (3%)
  starting transfers between devices  12.1 us (2%)
    unnamed x1, blocking collectives  278 us
    unnamed x2, waiting for transfers between devices  65.1 us
    psum x1, blocking collectives, per_device(): slots = lax.psum(jnp.concatenate([err_part, pow_part], axis=1), 'tensor')  45.7 us
    all_to_all x1, blocking collectives, per_device(): lax.all_to_all(outgoing, 'expert', split_axis=0, concat_axis=0, tiled=True)  34.8 us
  transfers between devices with their start and end apart: 3, of which 2 were waited for; matrix products, arithmetic and copies ran while one was open for 2% of the time, Pallas kernels for 0%

profile of v1, /device:TPU:2, one launch (start us, length us, event | category | flops | bytes accessed | tf_op | source)
XLA Modules:
  0.0 501.2 jit_solution(15373669247956984422)
XLA Ops:
  7.2 0.0 copy-start
  7.2 0.0 reduce-scatter.4.cloned.1.call-start
  7.2 0.0 copy-start.3
  7.2 2.8 copy.53
  10.0 0.0 copy-start.2
  10.0 0.0 reduce-scatter.4.cloned.1.call-update
  10.0 0.0 copy-done.3
  10.0 0.1 copy.38
  10.1 0.1 eq.40
  10.2 0.1 eq.44
  10.3 1.2 reduce-window.6
  11.5 0.2 slice_reduce_fusion
  11.7 0.2 fusion.20
  11.9 0.1 reduce_sum.93
  12.0 0.1 copy.41
  12.1 0.1 copy.42
  12.1 0.5 convert_reduce_fusion
  12.7 65.1 %reduce-scatter.4.cloned.1.call-done = bf16[448,64]{1,0:T(8,128)(2,1)} async-done(((bf16[7168,64]{1,0:T(8,128)(2,1)}), bf16[448,64]{1,0:T(8,128)(2,1)}) %reduce-scatter.4.cloned.1.call-update) | async-done | bytes 57360
  77.8 1.0 copy.54
  78.8 0.0 copy-done.2
  78.8 0.4 convolution_convert_fusion
  79.2 0.3 copy.43
  79.5 0.1 broadcast_in_dim.6
  79.6 0.2 pad_maximum_fusion
  79.8 34.8 %all_to_all.15 = bf16[32,25,448]{2,1,0:T(8,128)(2,1)S(1)} all-to-all(bf16[32,25,448]{2,1,0:T(8,128)(2,1)S(1)} %pad_maximum_fusion), channel_id=1, replica_groups=mesh['expert'=32,'tensor'=16] {'expert'}, dimensions={0} | all-to-all | bytes 1433600 | tf_op jit(solution)/shard_map/all_to_all | solution.py:42
  114.5 0.0 copy-start.1
  114.5 1.0 copy-done.1
  115.5 0.1 slice.37
  115.6 0.3 copy.44
  115.9 5.1 %stack.3 = bf16[16,768,448]{1,2,0:T(8,128)(2,1)} broadcast(bf16[768,448]{0,1:T(8,128)(2,1)S(1)} %copy.44), dimensions={1,2} | broadcast | bytes 11698176 | tf_op jit(solution)/shard_map/stack | solution.py:46
  121.0 0.0 copy-start.5
  121.0 6.5 %all-to-all-start.1 = ((bf16[16,768,448]{1,2,0:T(8,128)(2,1)}), bf16[16,768,448]{1,2,0:T(8,128)(2,1)}, u32[]{:S(2)}, u32[]{:S(2)}) async-start(bf16[16,768,448]{1,2,0:T(8,128)(2,1)} %stack.3), calls=%async_computation.1 | async-start | bytes 22020096 | tf_op jit(solution)/shard_map/all_to_all | solution.py:46
  127.5 0.0 copy-done.5
  127.6 1.3 dynamic-slice
  129.5 0.3 dynamic-update-slice
  129.8 278.2 %all-reduce = bf16[7168]{0:T(1024)(128)(2,1)S(1)} all-reduce(bf16[7168]{0:T(1024)(128)(2,1)S(1)} %dynamic-update-slice), channel_id=1, replica_groups=mesh['expert'=32,'tensor'=16] {'tensor'}, use_global_device_ids=true, to_apply=%add | all-reduce | flops 7168 | bytes 28672
  407.9 0.1 reshape.133
  408.0 0.0 copy-done.4
  408.0 0.1 copy.46
  408.1 1.5 fusion.22
  409.6 0.0 all-to-all-done.1
  409.6 6.4 %fusion = f32[768]{0:T(1024)S(1)} fusion(bf16[16,768,448]{1,2,0:T(8,128)(2,1)} %all-to-all-done.1), kind=kLoop, calls=%fused_computation.4 | loop fusion | flops 16514304 | bytes 11013120 | tf_op jit(solution)/shard_map/reduce_sum | solution.py:49
  416.0 0.4 fusion.7
  416.4 6.8 %fusion.2 = bf16[16,768,448]{1,2,0:T(8,128)(2,1)S(1)} fusion(bf16[16,768,448]{1,2,0:T(8,128)(2,1)} %all-to-all-done.1, f32[16,448]{1,0:T(8,128)S(1)} %reshape.133, f32[768]{0:T(1024)S(1)} %add_rsqrt_fusion), kind=kLoop, calls=%fused_computation.6 | loop fusion | flops 22020096 | bytes 22051840 | tf_op jit(solution)/shard_map/convert_element_type | solution.py:50
  423.2 0.0 copy-done
  423.2 0.0 copy-start.6
  423.2 1.8 multiply_reduce_fusion
  425.1 0.0 copy-done.6
  425.1 1.8 fusion.14
  426.9 0.1 div.34
  427.0 0.1 div.36
  427.1 45.7 %psum.7 = f32[32,2,24]{2,0,1:T(8,128)S(1)} all-reduce(f32[32,2,24]{2,0,1:T(8,128)S(1)} %pad_maximum_fusion.1), channel_id=1, replica_groups=mesh['expert'=32,'tensor'=16] {'tensor'}, use_global_device_ids=true, to_apply=%region_9.10 | all-reduce | flops 1536 | bytes 12288 | tf_op jit(solution)/shard_map/psum | solution.py:62
  472.8 0.6 copy.45
  473.4 5.6 %all-to-all-start.2 = ((f32[32,2,24]{2,1,0:T(2,128)}), f32[32,2,24]{2,1,0:T(2,128)S(1)}, u32[]{:S(2)}, u32[]{:S(2)}) async-start(f32[32,2,24]{2,1,0:T(2,128)} %copy.45), calls=%async_computation.2 | async-start | bytes 65536 | tf_op jit(solution)/shard_map/all_to_all | solution.py:64
  479.0 1.2 multiply_divide_fusion
  480.2 0.6 slice_reduce_fusion.1
  482.2 5.5 %all-to-all-done.2 = f32[32,2,24]{2,1,0:T(2,128)S(1)} async-done(((f32[32,2,24]{2,1,0:T(2,128)}), f32[32,2,24]{2,1,0:T(2,128)S(1)}, u32[]{:S(2)}, u32[]{:S(2)}) %all-to-all-start.2) | async-done | bytes 6176 | tf_op jit(solution)/shard_map/all_to_all | solution.py:64
  487.6 0.1 slice_reduce_fusion.4
  487.7 0.1 reshape_squeeze.6
  487.8 0.1 reshape_squeeze.7
  487.9 2.3 gather_fusion
  490.2 2.3 gather_fusion.1
  492.5 0.1 div.38
  492.6 0.6 multiply_reduce_fusion.1
  (15 shorter events, 0.1 us)
Async XLA Ops:
  7.2 416.0 %copy-start = (bf16[1,7168,128]{2,1,0:T(8,128)(2,1)S(1)}, bf16[1,7168,128]{2,1,0:T(8,128)(2,1)}, u32[]{:S(2)}) copy-start(bf16[1,7168,128]{2,1,0:T(8,128)(2,1)} %param.14) | copy-start | bytes 5505028
  7.2 70.6 %reduce-scatter.4.cloned.1.call-start = ((), (), s32[]{:S(2)}) async-start(), calls=%async_computation.4 | async-start | bytes 1949696
  7.2 2.8 copy-start.3
  10.0 68.8 %copy-start.2 = (bf16[64,448]{1,0:T(8,128)(2,1)S(1)}, bf16[64,448]{1,0:T(8,128)(2,1)}, u32[]{:S(2)}) copy-start(bf16[64,448]{1,0:T(8,128)(2,1)} %param.9) | copy-start | bytes 172036
  114.5 1.0 copy-start.1
  121.0 6.6 %copy-start.5 = (bf16[448]{0:T(512)(128)(2,1)S(1)}, bf16[448]{0:T(512)(128)(2,1)}, u32[]{:S(2)}) copy-start(bf16[448]{0:T(512)(128)(2,1)} %param.11) | copy-start | bytes 2692
  121.0 287.1 %copy-start.4 = (f32[64,8]{0,1:T(8,128)S(1)}, f32[64,8]{0,1:T(8,128)}, u32[]{:S(2)}) copy-start(f32[64,8]{0,1:T(8,128)} %param.13) | copy-start | bytes 6148
  121.0 288.6 %all-to-all-start.1 = ((bf16[16,768,448]{1,2,0:T(8,128)(2,1)}), bf16[16,768,448]{1,2,0:T(8,128)(2,1)}, u32[]{:S(2)}, u32[]{:S(2)}) async-start(bf16[16,768,448]{1,2,0:T(8,128)(2,1)} %stack.3), calls=%async_computation.1 | async-start | bytes 22020096 | tf_op jit(solution)/shard_map/all_to_all | solution.py:46
  423.2 1.9 copy-start.6
  473.4 14.2 %all-to-all-start.2 = ((f32[32,2,24]{2,1,0:T(2,128)}), f32[32,2,24]{2,1,0:T(2,128)S(1)}, u32[]{:S(2)}, u32[]{:S(2)}) async-start(f32[32,2,24]{2,1,0:T(2,128)} %copy.45), calls=%async_computation.2 | async-start | bytes 65536 | tf_op jit(solution)/shard_map/all_to_all | solution.py:64
Sparse Core Ops, SparseCore 0:
  10.8 66.8 reduce-scatter.3
